TPU v7x, 32 devices: a whole 2x2x4 slice. The times are simulated.
32 devices in a mesh: grp: 8 (over z, y), col: 4 (over x, core).
Axes of the slice: x: 2, y: 2, z: 4, core: 2. Of those that a mesh axis runs over, the one named last changes fastest.
Arguments:
- right_side: float32 [256, 64, 128], P('grp', 'col'), may hold values from -6 to 6
- conductance: float32 [256, 64, 128], P('grp', 'col'), may hold values from 0.3 to 3
- reaction: float32 [256, 64, 128], P('grp', 'col'), may hold values from 0.05 to 0.5
- geneo: bfloat16 [6, 256, 64, 128], P(None, 'grp', 'col'), may hold values from -0.0234375 to 0.0234375
- coarse_inverse: float32 [8, 24, 24], P('grp'), as said below
Outputs:
- solution: float32 [256, 64, 128], P('grp', 'col')
- residual: float32 [256, 64, 128], P('grp', 'col')
Inputs may be any that keep to these rules, and one draw needn't show every extreme that they name: `coarse_inverse`: for each first-dimension block, a dense matrix of order 24.
All inputs are finite; a program needn't handle non-finite values.
Results may differ from a plain program's by a relative error of at most 0.0003.
Values sent between devices are 32-bit elements; how exact they have to be, the bound alone decides.
A program may use at most 64 MiB of HBM per device.

v0:
```python
import jax
import jax.numpy as jnp
from jax import lax
from jax.sharding import PartitionSpec as P

OV = 2
SWEEPS = 3


highest = lax.Precision.HIGHEST


def padded_2(cells, sides, width):
    for axis, dim in sides:
        count = lax.axis_size(axis)
        ends = count - 1
        head = lax.slice_in_dim(cells, 0, width, axis=dim)
        tail = lax.slice_in_dim(cells, cells.shape[dim] - width, cells.shape[dim], axis=dim)
        cells = jnp.concatenate(
            [
                lax.ppermute(tail, axis, [(i, (i + 1) % count) for i in range(ends)]),
                cells,
                lax.ppermute(head, axis, [((i + 1) % count, i) for i in range(ends)]),
            ],
            axis=dim,
        )
    return cells


def face_terms(k_rim, s_mid):
    centre = k_rim[1:-1, 1:-1]
    k_depth = jnp.pad(centre, ((0, 0), (0, 0), (1, 1)))
    west = 0.5 * (centre + k_rim[:-2, 1:-1])
    east = 0.5 * (centre + k_rim[2:, 1:-1])
    south = 0.5 * (centre + k_rim[1:-1, :-2])
    north = 0.5 * (centre + k_rim[1:-1, 2:])
    below = 0.5 * (centre + k_depth[:, :, :-2])
    above = 0.5 * (centre + k_depth[:, :, 2:])
    diagonal = s_mid + west + east + south + north + below + above
    return (west, east, south, north, below, above, diagonal)


def apply_faces(terms, padded):
    west, east, south, north, below, above, diagonal = terms
    middle = padded[1:-1, 1:-1]
    depth = jnp.pad(middle, ((0, 0), (0, 0), (1, 1)))
    beside_all = west * padded[:-2, 1:-1] + east * padded[2:, 1:-1]
    beside_all = beside_all + south * padded[1:-1, :-2] + north * padded[1:-1, 2:]
    beside_all = beside_all + below * depth[:, :, :-2] + above * depth[:, :, 2:]
    return diagonal * middle - beside_all


def local_solve(terms, inside, source):
    inverse = inside / jnp.where(inside > 0, terms[6], 1.0)
    guess = jnp.zeros_like(source)
    for sweep in range(SWEEPS):
        padded = jnp.pad(guess, ((1, 1), (1, 1), (0, 0)))
        guess = guess + inverse * (source - apply_faces(terms, padded))
    return guess


def margins(fields, width):
    rows = padded_2(fields, (("grp", 1),), width)
    return padded_2(rows, (("col", 2),), width)


def products(values):
    return lax.psum(values, ("grp", "col"))


def squared(value):
    return lax.psum(value, ("grp", "col"))


def interior(field):
    return field[OV:-OV, OV:-OV]


def body(right_side, conductance, reaction, geneo, coarse_inverse):
    size_x, size_y, size_z = right_side.shape
    stacked = jnp.stack([conductance, reaction, right_side])
    rimmed = margins(stacked, OV + 1)
    k_rim = rimmed[0]
    s_wide = rimmed[1, 1:-1, 1:-1]
    b_wide = rimmed[2, 1:-1, 1:-1]
    wide_terms = face_terms(k_rim, s_wide)
    own_terms = face_terms(k_rim[OV:-OV, OV:-OV], reaction)
    x_index = lax.axis_index("grp") * size_x - OV + jnp.arange(size_x + 2 * OV, dtype=jnp.int32)
    y_index = lax.axis_index("col") * size_y - OV + jnp.arange(size_y + 2 * OV, dtype=jnp.int32)
    x_valid = ((x_index >= 0) & (x_index < lax.axis_size("grp") * size_x)).astype(jnp.float32)
    y_valid = ((y_index >= 0) & (y_index < lax.axis_size("col") * size_y)).astype(jnp.float32)
    inside = x_valid[:, None, None] * y_valid[None, :, None] * jnp.ones((1, 1, size_z), jnp.float32)
    vectors = geneo.astype(jnp.float32)
    count = vectors.shape[0]
    own_rows = lax.dynamic_slice_in_dim(coarse_inverse[0], lax.axis_index("col") * count, count, 0)

    def precondition(source):
        local_part = interior(local_solve(wide_terms, inside, source))
        restricted = jnp.einsum("kxyz,xyz->k", vectors, interior(source), precision=highest)
        gathered = lax.all_gather(restricted, "col", axis=0, tiled=True)
        coarse = jnp.dot(own_rows, gathered, precision=highest)
        return local_part + jnp.einsum("k,kxyz->xyz", coarse, vectors, precision=highest)

    def image(field):
        padded = margins(field[None], 1)[0]
        return (apply_faces(own_terms, padded), field)

    z_raw = precondition(b_wide)
    w_raw, w_raw_wide = image(z_raw)
    totals = products(jnp.stack([jnp.sum(right_side * right_side), jnp.sum(right_side * w_raw)]))
    bb = totals[0]
    h11 = totals[1] / bb
    beta = jnp.sqrt(bb)
    w_one = (w_raw - h11 * right_side) / beta
    h21 = jnp.sqrt(squared(jnp.sum(w_one * w_one)))
    first = right_side / beta
    z_one = z_raw / beta
    second = (w_raw - h11 * right_side) / beta / h21
    second_wide = margins(second[None], OV)[0]
    z_two = precondition(second_wide)
    w_two, unused = image(z_two)
    totals = products(jnp.stack([jnp.sum(first * w_two), jnp.sum(second * w_two)]))
    h12 = totals[0]
    h22 = totals[1]
    rest = w_two - h12 * first - h22 * second
    h32 = jnp.sqrt(squared(jnp.sum(rest * rest)))
    third = rest / h32
    g11 = h11 * h11 + h21 * h21
    g12 = h11 * h12 + h21 * h22
    g22 = h12 * h12 + h22 * h22 + h32 * h32
    rhs_one = beta * h11
    rhs_two = beta * h12
    determinant = g11 * g22 - g12 * g12
    y_one = (g22 * rhs_one - g12 * rhs_two) / determinant
    y_two = (g11 * rhs_two - g12 * rhs_one) / determinant
    solution = y_one * z_one + y_two * z_two
    left_one = beta - h11 * y_one - h12 * y_two
    left_two = -h21 * y_one - h22 * y_two
    left_three = -h32 * y_two
    residual = left_one * first + left_two * second + left_three * third
    return (solution, residual)


def solution(mesh):
    return jax.shard_map(
        body,
        mesh=mesh,
        in_specs=(
            P("grp", "col", None),
            P("grp", "col", None),
            P("grp", "col", None),
            P(None, "grp", "col", None),
            P("grp", None, None),
        ),
        out_specs=(P("grp", "col", None), P("grp", "col", None)),
        check_vma=False,
    )
```

profile of v0, /device:TPU:0, one launch (start us, length us, event | category | flops | bytes accessed | tf_op | source)
XLA Modules:
  0.0 300.0 jit_solution(11826794244033402529)
XLA Ops:
  1.6 4.9 %collective-permute-start = (f32[3,3,16,128]{3,2,1,0:T(8,128)S(1)}, f32[3,3,16,128]{3,2,1,0:T(8,128)S(1)}, u32[]{:S(2)}, u32[]{:S(2)}) collective-permute-start(f32[3,3,16,128]{3,2,1,0:T(8,128)S(1)} %get-tuple-element.21), channel_id=1, source_target_pairs={{0,4},{4,8},{8,12},{12,16},{16,20},{20,24},{24,28},{1,5},{5,9},{9,... | collective-permute-start | bytes 221192 | tf_op jit(solution)/shard_map/ppermute | solution.py:21
  6.5 1.3 collective-permute-start.1
  8.5 1.2 dynamic-slice.1
  10.5 2.3 collective-permute-done.1
  12.8 1.3 pad_maximum_fusion.5
  14.1 1.3 collective-permute-start.2
  15.4 1.3 collective-permute-start.3
  16.8 3.7 %collective-permute-done.3 = f32[3,38,3,128]{3,2,1,0:T(4,128)S(1)} collective-permute-done((f32[3,38,3,128]{3,2,1,0:T(4,128)S(1)}, f32[3,38,3,128]{3,2,1,0:T(4,128)S(1)}, u32[]{:S(2)}, u32[]{:S(2)}) %collective-permute-start.3) | collective-permute-done | bytes 175136 | tf_op jit(solution)/shard_map/ppermute | solution.py:23
  21.8 1.8 select_divide_fusion
  23.6 1.8 subtract_multiply_fusion.1
  26.2 1.4 multiply_add_fusion.1
  27.6 3.2 %convolution_bitcast_fusion.1 = f32[6]{0:T(128)} fusion(f32[32,16,128,1]{2,3,1,0:T(1,128)S(1)} %bitcast.118, bf16[6,32,16,128]{3,2,1,0:T(8,128)(2,1)S(1)} %copy-done), kind=kOutput, calls=%fused_computation.4 | convolution fusion | flops 4718592 | bytes 1048600 | tf_op jit(solution)/shard_map/kxyz,xyz->k/dot_general | solution.py:99
  31.3 1.3 dynamic-update-slice
  32.6 10.8 %all-reduce.14 = f32[24]{0:T(128)} all-reduce(f32[24]{0:T(128)} %dynamic-update-slice), channel_id=1, replica_groups=mesh['grp'=8,'col'=4] {'col'}, use_global_device_ids=true, to_apply=%add.14 | all-reduce | flops 24 | bytes 192
  45.5 1.8 fusion.89
  47.3 4.3 %collective-permute-start.4 = (f32[1,1,16,128]{3,2,1,0:T(8,128)S(1)}, f32[1,1,16,128]{3,2,1,0:T(8,128)S(1)}, u32[]{:S(2)}, u32[]{:S(2)}) collective-permute-start(f32[1,1,16,128]{3,2,1,0:T(8,128)S(1)} %get-tuple-element.39), channel_id=1, source_target_pairs={{0,4},{4,8},{8,12},{12,16},{16,20},{20,24},{24,28},{1,5},{5,9},{9,... | collective-permute-start | bytes 24584 | tf_op jit(solution)/shard_map/ppermute | solution.py:21
  51.6 1.3 collective-permute-start.5
  53.0 4.2 %collective-permute-done.5 = f32[1,1,16,128]{3,2,1,0:T(8,128)S(1)} collective-permute-done((f32[1,1,16,128]{3,2,1,0:T(8,128)S(1)}, f32[1,1,16,128]{3,2,1,0:T(8,128)S(1)}, u32[]{:S(2)}, u32[]{:S(2)}) %collective-permute-start.5) | collective-permute-done | bytes 8224 | tf_op jit(solution)/shard_map/ppermute | solution.py:23
  57.2 1.3 collective-permute-start.6
  58.5 1.3 collective-permute-start.7
  59.8 3.6 %collective-permute-done.7 = f32[1,34,1,128]{3,2,1,0:T(1,128)S(1)} collective-permute-done((f32[1,34,1,128]{3,2,1,0:T(1,128)S(1)}, f32[1,34,1,128]{3,2,1,0:T(1,128)S(1)}, u32[]{:S(2)}, u32[]{:S(2)}) %collective-permute-start.7) | collective-permute-done | bytes 17440 | tf_op jit(solution)/shard_map/ppermute | solution.py:23
  63.5 1.8 multiply_reduce_fusion.5
  65.4 1.5 pad_maximum_fusion.18
  66.8 41.4 %psum.28 = f32[2]{0:T(128)S(1)} all-reduce(f32[2]{0:T(128)S(1)} %pad_maximum_fusion.18), channel_id=1, replica_groups=mesh['grp'=8,'col'=4] {'grp','col'}, use_global_device_ids=true, to_apply=%region_2.3 | all-reduce | flops 2 | bytes 16 | tf_op jit(solution)/shard_map/psum | solution.py:68
  111.0 1.7 multiply_reduce_fusion.3
  112.8 38.9 %psum.29 = f32[]{:T(128)} all-reduce(f32[]{:T(128)} %multiply_reduce_fusion.3), channel_id=1, replica_groups=mesh['grp'=8,'col'=4] {'grp','col'}, use_global_device_ids=true, to_apply=%region_4.5 | all-reduce | flops 1 | bytes 8 | tf_op jit(solution)/shard_map/psum | solution.py:72
  153.5 4.4 %collective-permute-start.8 = (f32[1,2,16,128]{3,2,1,0:T(8,128)S(1)}, f32[1,2,16,128]{3,2,1,0:T(8,128)S(1)}, u32[]{:S(2)}, u32[]{:S(2)}) collective-permute-start(f32[1,2,16,128]{3,2,1,0:T(8,128)S(1)} %get-tuple-element.37), channel_id=1, source_target_pairs={{0,4},{4,8},{8,12},{12,16},{16,20},{20,24},{24,28},{1,5},{5,9},{9,... | collective-permute-start | bytes 49160 | tf_op jit(solution)/shard_map/ppermute | solution.py:21
  158.0 1.3 collective-permute-start.9
  159.4 4.2 %collective-permute-done.9 = f32[1,2,16,128]{3,2,1,0:T(8,128)S(1)} collective-permute-done((f32[1,2,16,128]{3,2,1,0:T(8,128)S(1)}, f32[1,2,16,128]{3,2,1,0:T(8,128)S(1)}, u32[]{:S(2)}, u32[]{:S(2)}) %collective-permute-start.9) | collective-permute-done | bytes 16416 | tf_op jit(solution)/shard_map/ppermute | solution.py:23
  163.7 1.3 collective-permute-start.10
  165.0 1.5 collective-permute-start.11
  166.5 3.4 %collective-permute-done.11 = f32[1,36,2,128]{3,2,1,0:T(2,128)S(1)} collective-permute-done((f32[1,36,2,128]{3,2,1,0:T(2,128)S(1)}, f32[1,36,2,128]{3,2,1,0:T(2,128)S(1)}, u32[]{:S(2)}, u32[]{:S(2)}) %collective-permute-start.11) | collective-permute-done | bytes 36896 | tf_op jit(solution)/shard_map/ppermute | solution.py:23
  169.8 1.3 subtract_multiply_fusion
  171.9 1.4 multiply_add_fusion
  174.1 2.7 convolution_bitcast_fusion
  177.0 8.3 %all-reduce.15 = f32[24]{0:T(128)S(1)} all-reduce(f32[24]{0:T(128)S(1)} %dynamic-update-slice.1), channel_id=1, replica_groups=mesh['grp'=8,'col'=4] {'col'}, use_global_device_ids=true, to_apply=%add.15 | all-reduce | flops 24 | bytes 192
  187.4 1.7 fusion.80
  189.2 4.4 %collective-permute-start.12 = (f32[1,1,16,128]{3,2,1,0:T(8,128)S(1)}, f32[1,1,16,128]{3,2,1,0:T(8,128)S(1)}, u32[]{:S(2)}, u32[]{:S(2)}) collective-permute-start(f32[1,1,16,128]{3,2,1,0:T(8,128)S(1)} %get-tuple-element.35), channel_id=1, source_target_pairs={{0,4},{4,8},{8,12},{12,16},{16,20},{20,24},{24,28},{1,5},{5,9},{9,... | collective-permute-start | bytes 24584 | tf_op jit(solution)/shard_map/ppermute | solution.py:21
  193.6 1.3 collective-permute-start.13
  194.9 4.2 %collective-permute-done.13 = f32[1,1,16,128]{3,2,1,0:T(8,128)S(1)} collective-permute-done((f32[1,1,16,128]{3,2,1,0:T(8,128)S(1)}, f32[1,1,16,128]{3,2,1,0:T(8,128)S(1)}, u32[]{:S(2)}, u32[]{:S(2)}) %collective-permute-start.13) | collective-permute-done | bytes 8224 | tf_op jit(solution)/shard_map/ppermute | solution.py:23
  199.1 1.3 collective-permute-start.14
  200.4 1.3 collective-permute-start.15
  201.8 3.6 %collective-permute-done.15 = f32[1,34,1,128]{3,2,1,0:T(1,128)S(1)} collective-permute-done((f32[1,34,1,128]{3,2,1,0:T(1,128)S(1)}, f32[1,34,1,128]{3,2,1,0:T(1,128)S(1)}, u32[]{:S(2)}, u32[]{:S(2)}) %collective-permute-start.15) | collective-permute-done | bytes 17440 | tf_op jit(solution)/shard_map/ppermute | solution.py:23
  206.6 1.4 pad_maximum_fusion.19
  208.0 41.2 %psum.30 = f32[2]{0:T(128)S(1)} all-reduce(f32[2]{0:T(128)S(1)} %pad_maximum_fusion.19), channel_id=1, replica_groups=mesh['grp'=8,'col'=4] {'grp','col'}, use_global_device_ids=true, to_apply=%region_7.8 | all-reduce | flops 2 | bytes 16 | tf_op jit(solution)/shard_map/psum | solution.py:68
  253.8 2.0 multiply_reduce_fusion
  256.5 39.1 %psum.31 = f32[]{:T(128)} all-reduce(f32[]{:T(128)} %multiply_reduce_fusion), channel_id=1, replica_groups=mesh['grp'=8,'col'=4] {'grp','col'}, use_global_device_ids=true, to_apply=%region_9.10 | all-reduce | flops 1 | bytes 8 | tf_op jit(solution)/shard_map/psum | solution.py:72
  297.7 2.3 multiply_add_fusion.2
  (106 shorter events, 14.1 us)
Async XLA Ops:
  0.6 27.0 %copy-start = (bf16[6,32,16,128]{3,2,1,0:T(8,128)(2,1)S(1)}, bf16[6,32,16,128]{3,2,1,0:T(8,128)(2,1)}, u32[]{:S(2)}) copy-start(bf16[6,32,16,128]{3,2,1,0:T(8,128)(2,1)} %param.8) | copy-start | bytes 2359300
  0.6 19.9 %copy-start.12 = (f32[32,16,128]{2,1,0:T(8,128)S(1)}, f32[32,16,128]{2,1,0:T(8,128)}, u32[]{:S(2)}) copy-start(f32[32,16,128]{2,1,0:T(8,128)} %param.6) | copy-start | bytes 786436
  0.7 19.9 %copy-start.6 = (f32[32,16,128]{2,1,0:T(8,128)S(1)}, f32[32,16,128]{2,1,0:T(8,128)}, u32[]{:S(2)}) copy-start(f32[32,16,128]{2,1,0:T(8,128)} %param.7) | copy-start | bytes 786436
  0.7 19.9 %copy-start.1 = (f32[32,16,128]{2,1,0:T(8,128)S(1)}, f32[32,16,128]{2,1,0:T(8,128)}, u32[]{:S(2)}) copy-start(f32[32,16,128]{2,1,0:T(8,128)} %param.5) | copy-start | bytes 786436
  1.6 8.8 %collective-permute-start = (f32[3,3,16,128]{3,2,1,0:T(8,128)S(1)}, f32[3,3,16,128]{3,2,1,0:T(8,128)S(1)}, u32[]{:S(2)}, u32[]{:S(2)}) collective-permute-start(f32[3,3,16,128]{3,2,1,0:T(8,128)S(1)} %get-tuple-element.21), channel_id=1, source_target_pairs={{0,4},{4,8},{8,12},{12,16},{16,20},{20,24},{24,28},{1,5},{5,9},{9,... | collective-permute-start | bytes 221192 | tf_op jit(solution)/shard_map/ppermute | solution.py:21
  6.5 6.2 %collective-permute-start.1 = (f32[3,3,16,128]{3,2,1,0:T(8,128)S(1)}, f32[3,3,16,128]{3,2,1,0:T(8,128)S(1)}, u32[]{:S(2)}, u32[]{:S(2)}) collective-permute-start(f32[3,3,16,128]{3,2,1,0:T(8,128)S(1)} %get-tuple-element.22), channel_id=1, source_target_pairs={{4,0},{8,4},{12,8},{16,12},{20,16},{24,20},{28,24},{5,1},{9,5},{13... | collective-permute-start | bytes 221192 | tf_op jit(solution)/shard_map/ppermute | solution.py:23
  10.4 10.1 %copy-start.25 = (f32[3,3,16,128]{3,2,1,0:T(8,128)}, f32[3,3,16,128]{3,2,1,0:T(8,128)S(1)}, u32[]{:S(2)}) copy-start(f32[3,3,16,128]{3,2,1,0:T(8,128)S(1)} %collective-permute-done) | copy-start | bytes 221188
  12.8 7.7 %copy-start.27 = (f32[3,3,16,128]{3,2,1,0:T(8,128)}, f32[3,3,16,128]{3,2,1,0:T(8,128)S(1)}, u32[]{:S(2)}) copy-start(f32[3,3,16,128]{3,2,1,0:T(8,128)S(1)} %collective-permute-done.1) | copy-start | bytes 221188
  14.1 2.7 collective-permute-start.2
  15.4 5.1 %collective-permute-start.3 = (f32[3,38,3,128]{3,2,1,0:T(4,128)S(1)}, f32[3,38,3,128]{3,2,1,0:T(4,128)S(1)}, u32[]{:S(2)}, u32[]{:S(2)}) collective-permute-start(f32[3,38,3,128]{3,2,1,0:T(4,128)S(1)} %get-tuple-element.20), channel_id=1, source_target_pairs={{1,0},{2,1},{3,2},{5,4},{6,5},{7,6},{9,8},{10,9},{11,10},{13,12},{... | collective-permute-start | bytes 525320 | tf_op jit(solution)/shard_map/ppermute | solution.py:23
  20.8 1.0 copy-start.13
  20.8 1.0 copy-start.26
  20.8 1.0 copy-start.28
  20.8 1.0 copy-start.29
  23.6 1.9 copy-start.8
  23.6 2.5 copy-start.2
  23.6 2.5 copy-start.4
  25.4 0.8 copy-start.14
  26.2 1.4 copy-start.20
  43.4 2.1 copy-start.9
  43.4 2.1 copy-start.15
  47.3 16.2 %copy-start.16 = (f32[32,16,128]{2,1,0:T(8,128)}, f32[32,16,128]{2,1,0:T(8,128)S(1)}, u32[]{:S(2)}) copy-start(f32[32,16,128]{2,1,0:T(8,128)S(1)} %fusion.89) | copy-start | bytes 786436
  47.3 5.7 %collective-permute-start.4 = (f32[1,1,16,128]{3,2,1,0:T(8,128)S(1)}, f32[1,1,16,128]{3,2,1,0:T(8,128)S(1)}, u32[]{:S(2)}, u32[]{:S(2)}) collective-permute-start(f32[1,1,16,128]{3,2,1,0:T(8,128)S(1)} %get-tuple-element.39), channel_id=1, source_target_pairs={{0,4},{4,8},{8,12},{12,16},{16,20},{20,24},{24,28},{1,5},{5,9},{9,... | collective-permute-start | bytes 24584 | tf_op jit(solution)/shard_map/ppermute | solution.py:21
  51.6 5.5 %collective-permute-start.5 = (f32[1,1,16,128]{3,2,1,0:T(8,128)S(1)}, f32[1,1,16,128]{3,2,1,0:T(8,128)S(1)}, u32[]{:S(2)}, u32[]{:S(2)}) collective-permute-start(f32[1,1,16,128]{3,2,1,0:T(8,128)S(1)} %get-tuple-element.40), channel_id=1, source_target_pairs={{4,0},{8,4},{12,8},{16,12},{20,16},{24,20},{28,24},{5,1},{9,5},{13... | collective-permute-start | bytes 24584 | tf_op jit(solution)/shard_map/ppermute | solution.py:23
  57.2 2.6 collective-permute-start.6
  58.5 4.9 %collective-permute-start.7 = (f32[1,34,1,128]{3,2,1,0:T(1,128)S(1)}, f32[1,34,1,128]{3,2,1,0:T(1,128)S(1)}, u32[]{:S(2)}, u32[]{:S(2)}) collective-permute-start(f32[1,34,1,128]{3,2,1,0:T(1,128)S(1)} %get-tuple-element.34), channel_id=1, source_target_pairs={{1,0},{2,1},{3,2},{5,4},{6,5},{7,6},{9,8},{10,9},{11,10},{13,12},{... | collective-permute-start | bytes 52232 | tf_op jit(solution)/shard_map/ppermute | solution.py:23
  59.8 5.6 %copy-start.21 = (f32[32,16,128]{2,1,0:T(8,128)}, f32[32,16,128]{2,1,0:T(8,128)S(1)}, u32[]{:S(2)}) copy-start(f32[32,16,128]{2,1,0:T(8,128)S(1)} %slice.362) | copy-start | bytes 786436
  152.4 18.7 %copy-start.3 = (f32[36,20,128]{2,1,0:T(8,128)S(1)}, f32[36,20,128]{2,1,0:T(8,128)}, u32[]{:S(2)}) copy-start(f32[36,20,128]{2,1,0:T(8,128)} %copy-done.2) | copy-start | bytes 1105924
  152.4 18.7 %copy-start.5 = (f32[36,20,128]{2,1,0:T(8,128)S(1)}, f32[36,20,128]{2,1,0:T(8,128)}, u32[]{:S(2)}) copy-start(f32[36,20,128]{2,1,0:T(8,128)} %copy-done.4) | copy-start | bytes 1105924
  152.4 18.7 %copy-start.10 = (f32[36,20,128]{2,1,0:T(8,128)S(1)}, f32[36,20,128]{2,1,0:T(8,128)}, u32[]{:S(2)}) copy-start(f32[36,20,128]{2,1,0:T(8,128)} %copy-done.8) | copy-start | bytes 1105924
  152.4 18.7 %copy-start.30 = (f32[36,20]{1,0:T(8,128)S(1)}, f32[36,20]{1,0:T(8,128)}, u32[]{:S(2)}) copy-start(f32[36,20]{1,0:T(8,128)} %broadcast_multiply_fusion) | copy-start | bytes 8644
  153.5 5.9 %collective-permute-start.8 = (f32[1,2,16,128]{3,2,1,0:T(8,128)S(1)}, f32[1,2,16,128]{3,2,1,0:T(8,128)S(1)}, u32[]{:S(2)}, u32[]{:S(2)}) collective-permute-start(f32[1,2,16,128]{3,2,1,0:T(8,128)S(1)} %get-tuple-element.37), channel_id=1, source_target_pairs={{0,4},{4,8},{8,12},{12,16},{16,20},{20,24},{24,28},{1,5},{5,9},{9,... | collective-permute-start | bytes 49160 | tf_op jit(solution)/shard_map/ppermute | solution.py:21
  158.0 5.6 %collective-permute-start.9 = (f32[1,2,16,128]{3,2,1,0:T(8,128)S(1)}, f32[1,2,16,128]{3,2,1,0:T(8,128)S(1)}, u32[]{:S(2)}, u32[]{:S(2)}) collective-permute-start(f32[1,2,16,128]{3,2,1,0:T(8,128)S(1)} %get-tuple-element.38), channel_id=1, source_target_pairs={{4,0},{8,4},{12,8},{16,12},{20,16},{24,20},{28,24},{5,1},{9,5},{13... | collective-permute-start | bytes 49160 | tf_op jit(solution)/shard_map/ppermute | solution.py:23
  163.7 2.8 collective-permute-start.10
  165.0 4.8 %collective-permute-start.11 = (f32[1,36,2,128]{3,2,1,0:T(2,128)S(1)}, f32[1,36,2,128]{3,2,1,0:T(2,128)S(1)}, u32[]{:S(2)}, u32[]{:S(2)}) collective-permute-start(f32[1,36,2,128]{3,2,1,0:T(2,128)S(1)} %get-tuple-element.30), channel_id=1, source_target_pairs={{1,0},{2,1},{3,2},{5,4},{6,5},{7,6},{9,8},{10,9},{11,10},{13,12},{... | collective-permute-start | bytes 110600 | tf_op jit(solution)/shard_map/ppermute | solution.py:23
  171.9 1.4 copy-start.18
  173.4 0.8 copy-start.23
  174.1 13.2 %copy-start.11 = (f32[36,20,128]{2,1,0:T(8,128)S(1)}, f32[36,20,128]{2,1,0:T(8,128)}, u32[]{:S(2)}) copy-start(f32[36,20,128]{2,1,0:T(8,128)} %copy-done.8) | copy-start | bytes 1105924
  174.1 13.2 %copy-start.19 = (f32[36,20,128]{2,1,0:T(8,128)S(1)}, f32[36,20,128]{2,1,0:T(8,128)}, u32[]{:S(2)}) copy-start(f32[36,20,128]{2,1,0:T(8,128)} %copy-done.18) | copy-start | bytes 1105924
  185.3 2.1 copy-start.24
  189.1 16.4 %copy-start.7 = (f32[32,16,128]{2,1,0:T(8,128)S(1)}, f32[32,16,128]{2,1,0:T(8,128)}, u32[]{:S(2)}) copy-start(f32[32,16,128]{2,1,0:T(8,128)} %param.7) | copy-start | bytes 786436
  189.1 16.4 %copy-start.22 = (f32[32,16,128]{2,1,0:T(8,128)S(1)}, f32[32,16,128]{2,1,0:T(8,128)}, u32[]{:S(2)}) copy-start(f32[32,16,128]{2,1,0:T(8,128)} %copy-done.21) | copy-start | bytes 786436
  189.2 5.8 %collective-permute-start.12 = (f32[1,1,16,128]{3,2,1,0:T(8,128)S(1)}, f32[1,1,16,128]{3,2,1,0:T(8,128)S(1)}, u32[]{:S(2)}, u32[]{:S(2)}) collective-permute-start(f32[1,1,16,128]{3,2,1,0:T(8,128)S(1)} %get-tuple-element.35), channel_id=1, source_target_pairs={{0,4},{4,8},{8,12},{12,16},{16,20},{20,24},{24,28},{1,5},{5,9},{9,... | collective-permute-start | bytes 24584 | tf_op jit(solution)/shard_map/ppermute | solution.py:21
  193.6 5.5 %collective-permute-start.13 = (f32[1,1,16,128]{3,2,1,0:T(8,128)S(1)}, f32[1,1,16,128]{3,2,1,0:T(8,128)S(1)}, u32[]{:S(2)}, u32[]{:S(2)}) collective-permute-start(f32[1,1,16,128]{3,2,1,0:T(8,128)S(1)} %get-tuple-element.36), channel_id=1, source_target_pairs={{4,0},{8,4},{12,8},{16,12},{20,16},{24,20},{28,24},{5,1},{9,5},{13... | collective-permute-start | bytes 24584 | tf_op jit(solution)/shard_map/ppermute | solution.py:23
  199.1 2.6 collective-permute-start.14
  200.4 4.9 %collective-permute-start.15 = (f32[1,34,1,128]{3,2,1,0:T(1,128)S(1)}, f32[1,34,1,128]{3,2,1,0:T(1,128)S(1)}, u32[]{:S(2)}, u32[]{:S(2)}) collective-permute-start(f32[1,34,1,128]{3,2,1,0:T(1,128)S(1)} %get-tuple-element.32), channel_id=1, source_target_pairs={{1,0},{2,1},{3,2},{5,4},{6,5},{7,6},{9,8},{10,9},{11,10},{13,12},{... | collective-permute-start | bytes 52232 | tf_op jit(solution)/shard_map/ppermute | solution.py:23
  205.5 92.2 %copy-start.17 = (f32[32,16,128]{2,1,0:T(8,128)S(1)}, f32[32,16,128]{2,1,0:T(8,128)}, u32[]{:S(2)}) copy-start(f32[32,16,128]{2,1,0:T(8,128)} %copy-done.16) | copy-start | bytes 786436
where the time goes:
time: 301 us; the launch traced here: 300 us
  blocking collectives  180 us (60%)
  starting transfers between devices  33.8 us (11%)
  waiting for transfers between devices  29.4 us (10%)
  other arithmetic  28.9 us (10%)
  between operations  11.6 us (4%)
  matrix products  9.97 us (3%)
  local copies, waits for them, and re-layouts  6.63 us (2%)
    psum x2, blocking collectives, products(): return lax.psum(values, ('grp', 'col'))  82.6 us
    psum x2, blocking collectives, squared(): return lax.psum(value, ('grp', 'col'))  78 us
    ppermute x8, waiting for transfers between devices, padded_2(): lax.ppermute(head, axis, [((i + 1) % count, i) for i in range(ends)])  29.2 us
    ppermute x8, starting transfers between devices, padded_2(): lax.ppermute(tail, axis, [(i, (i + 1) % count) for i in range(ends)])  23.3 us
    unnamed x2, blocking collectives  19.1 us
    ppermute x8, starting transfers between devices, padded_2(): lax.ppermute(head, axis, [((i + 1) % count, i) for i in range(ends)])  10.5 us
  transfers between devices with their start and end apart: 16, of which 9 were waited for; matrix products, arithmetic and copies ran while one was open for 1% of the time, Pallas kernels for 0%

commit v1 on v0

v1 whole, which is shorter than its diff:
```python
import functools

import jax
import jax.numpy as jnp
from jax import lax
from jax.experimental import pallas as pl
from jax.experimental.pallas import tpu as pltpu
from jax.sharding import PartitionSpec as P

F32 = jnp.float32
MESH = pl.DeviceIdType.MESH
G = 3
T2 = 16
ROWS = 24


def loop(lo, hi, step, body, init=()):
    count = (hi - lo) // step

    def several(i, carry):
        for j in range(step):
            carry = body(lo + i * step + j, carry)
        return carry

    carry = lax.fori_loop(0, count, several, init)
    for x in range(lo + count * step, hi):
        carry = body(x, carry)
    return carry


def kernel(
    n_p, n_q, b_hbm, k_hbm, s_hbm, g_hbm, m_hbm, sol_hbm, res_hbm,
    K, S, B, Z1, Z2, W, U, V, EX, NY, SY, AZ, BZ, INV, D, Y2,
    geneo, minv, face_lo, face_hi, edge_p, edge_m,
    zs1, zr1, zs2, zr2, ws, wr, cs, cr,
    rc_out, rc1, rc2, c_scr, row_out, ar1, ar2, sol, res,
    load_sem, send_sem, recv_sem, all_sem,
):
    p = lax.axis_index("grp")
    q = lax.axis_index("col")
    nx = k_hbm.shape[0]
    nc = geneo.shape[0]
    ncs = minv.shape[1]
    n_all = n_p * n_q
    me = p * n_q + q
    last = G + nx
    own = pl.ds(G, nx)
    low = pl.ds(0, T2)
    f = slice(None)

    loads = []
    for i, (src, dst) in enumerate((
        (k_hbm, K.at[own, low]), (s_hbm, S.at[own, low]), (b_hbm, B.at[own, low]),
        (g_hbm, geneo), (m_hbm, minv),
    )):
        copy = pltpu.make_async_copy(src, dst, load_sem.at[i])
        copy.start()
        loads.append(copy)

    barrier = pltpu.get_barrier_semaphore()

    def other(t):
        dest = lax.rem(me + t, n_all)
        return (lax.div(dest, n_q), lax.rem(dest, n_q))

    def greet(t, carry):
        pl.semaphore_signal(barrier, inc=1, device_id=other(t), device_id_type=MESH)
        return carry

    lax.fori_loop(1, n_all, greet, 0)

    lane = lax.broadcasted_iota(jnp.int32, (1, 128), 1)
    sub = lax.broadcasted_iota(jnp.int32, (8, 128), 0)
    row = lax.broadcasted_iota(jnp.int32, (ROWS, 128), 0)

    counter = [0]

    def transfer(src, dst, dp, dq):
        i = counter[0]
        counter[0] += 1
        to_p, to_q = p + dp, q + dq
        from_p, from_q = p - dp, q - dq
        sends = (to_p >= 0) & (to_p < n_p) & (to_q >= 0) & (to_q < n_q)
        takes = (from_p >= 0) & (from_p < n_p) & (from_q >= 0) & (from_q < n_q)
        copy = pltpu.make_async_remote_copy(
            src_ref=src, dst_ref=dst, send_sem=send_sem.at[i], recv_sem=recv_sem.at[i],
            device_id=(to_p, to_q), device_id_type=MESH,
        )
        return copy, sends, takes, dst

    pending = []

    def start(items):
        for copy, sends, takes, dst in items:
            pl.when(sends)(copy.start)
            pending.append((copy, sends))

    def arrive(items):
        for copy, sends, takes, dst in items:
            pl.when(takes)(copy.wait_recv)

    def blank(items):
        for copy, sends, takes, dst in items:
            @pl.when(jnp.logical_not(takes))
            def _():
                dst[...] = jnp.zeros(dst.shape, F32)

    r1 = []
    for array, src, width in ((K, k_hbm, 3), (S, s_hbm, 2), (B, b_hbm, 2)):
        r1.append(transfer(src.at[pl.ds(nx - width, width)], array.at[pl.ds(G - width, width), low], 1, 0))
        r1.append(transfer(src.at[pl.ds(0, width)], array.at[pl.ds(last, width), low], -1, 0))
    r1.append(transfer(face_hi, edge_m.at[own], 0, 1))
    r1.append(transfer(face_lo, edge_p.at[own], 0, -1))
    for dp, here, there in ((1, pl.ds(nx - G, G), pl.ds(0, G)), (-1, pl.ds(0, G), pl.ds(last, G))):
        r1.append(transfer(face_hi.at[here], edge_m.at[there], dp, 1))
        r1.append(transfer(face_lo.at[here], edge_p.at[there], dp, -1))

    def z_round(Z, zs, zr):
        return [
            transfer(Z.at[last - 1, low], Z.at[G - 1, low], 1, 0),
            transfer(Z.at[G, low], Z.at[last, low], -1, 0),
            transfer(zs.at[1], zr.at[1], 0, 1),
            transfer(zs.at[0], zr.at[0], 0, -1),
        ]

    r2 = z_round(Z1, zs1, zr1)
    r4 = z_round(Z2, zs2, zr2)
    r3 = [
        transfer(W.at[pl.ds(last - 2, 2), low], W.at[pl.ds(G - 2, 2), low], 1, 0),
        transfer(W.at[pl.ds(G, 2), low], W.at[pl.ds(last, 2), low], -1, 0),
        transfer(ws.at[1], wr.at[1], 0, 1),
        transfer(ws.at[0], wr.at[0], 0, -1),
        transfer(cs.at[0], cr.at[0], 1, 1),
        transfer(cs.at[1], cr.at[1], 1, -1),
        transfer(cs.at[2], cr.at[2], -1, 1),
        transfer(cs.at[3], cr.at[3], -1, -1),
    ]
    for items in (r1, r2, r3, r4):
        blank(items)

    def spread(src, dst, i, devices):
        count, slot, where = devices

        def one(t):
            return pltpu.make_async_remote_copy(
                src_ref=src, dst_ref=dst.at[slot], send_sem=all_sem.at[2 * i], recv_sem=all_sem.at[2 * i + 1],
                device_id=where(t), device_id_type=MESH,
            )

        def go(t, carry):
            one(t).start()
            return carry

        lax.fori_loop(1, count, go, 0)
        dst[slot] = src[...]

        def whole():
            part = dst.at[pl.ds(0, count - 1)]
            return pltpu.make_async_remote_copy(
                src_ref=part, dst_ref=part, send_sem=all_sem.at[2 * i], recv_sem=all_sem.at[2 * i + 1],
                device_id=where(1), device_id_type=MESH,
            )

        return whole

    in_col = (n_q, q, lambda t: (p, lax.rem(q + t, n_q)))
    in_all = (n_all, me, other)

    def packed(parts, first_lane):
        tile = jnp.zeros((8, 128), F32)
        for i, part in enumerate(parts):
            tile = jnp.where(sub == i, jnp.sum(part, axis=0, keepdims=True), tile)
        sums = jnp.sum(tile, axis=1, keepdims=True)
        lanes = lax.broadcasted_iota(jnp.int32, (8, 128), 1)
        placed = jnp.where(lanes == sub + first_lane, sums, 0.0)
        return jnp.sum(jnp.where(sub < len(parts), placed, 0.0), axis=0, keepdims=True)

    def restrict(src):
        def step(x, carry):
            value = src[x, low]
            return tuple(acc + geneo[j, x - G].astype(F32) * value for j, acc in enumerate(carry))

        sums = loop(G, last, 2, step, tuple(jnp.zeros((T2, 128), F32) for _ in range(nc)))
        return packed(sums, q * nc)

    def coarse(rc):
        total = rc[0]
        for i in range(1, n_q):
            total = total + rc[i]
        c = jnp.sum(minv[0] * total[:, :ncs], axis=1, keepdims=True)
        c_scr[...] = jnp.broadcast_to(c, (ncs, 128))
        return [c_scr[pl.ds(q * nc + j, 1), :] for j in range(nc)]

    for copy in loads[:3]:
        copy.wait()

    def pack(x, carry):
        kl, sl, bl = K[x, 0:8], S[x, 0:8], B[x, 0:8]
        kt, st, bt = K[x, 8:16], S[x, 8:16], B[x, 8:16]
        face_lo[x - G] = jnp.where(sub < 3, kl, jnp.where(sub < 5, pltpu.roll(sl, 3, 0), pltpu.roll(bl, 5, 0)))
        face_hi[x - G] = jnp.where(sub > 4, kt, jnp.where(sub > 2, pltpu.roll(st, 5, 0), pltpu.roll(bt, 3, 0)))
        return carry

    loop(G, last, 4, pack)
    pl.semaphore_wait(barrier, n_all - 1)
    start(r1)
    loads[3].wait()
    loads[4].wait()
    rc_out[0] = restrict(B)
    rc_wait1 = spread(rc_out.at[0], rc1, 0, in_col)
    arrive(r1)

    def fill(x, carry):
        plus, minus = edge_p[x], edge_m[x]
        K[x, 16:24] = jnp.where(sub < 4, plus, minus)
        S[x, 16:24] = jnp.where(sub < 4, pltpu.roll(plus, 5, 0), pltpu.roll(minus, 3, 0))
        B[x, 16:24] = jnp.where(sub < 4, pltpu.roll(plus, 3, 0), pltpu.roll(minus, 5, 0))
        return carry

    loop(0, last + G, 2, fill)
    y_ok = (row < T2) | ((row < T2 + 2) & (q < n_q - 1)) | ((row >= ROWS - 2) & (q > 0))

    EX[0] = 0.5 * (K[0] + K[1])

    def terms(x, carry):
        kh = 0.5 * K[x]
        east = kh + 0.5 * K[x + 1]
        EX[x] = east
        north = kh + pltpu.roll(kh, ROWS - 1, 0)
        south = kh + pltpu.roll(kh, 1, 0)
        above = jnp.where(lane < 127, pltpu.roll(kh, 127, 1), 0.0)
        below = jnp.where(lane > 0, pltpu.roll(kh, 1, 1), 0.0)
        d = S[x] + east + EX[x - 1] + north + south + ((kh + above) + (kh + below))
        x_ok = ((x >= G) | (p > 0)) & ((x < last) | (p < n_p - 1))
        inv = jnp.where(y_ok & x_ok, 1.0 / d, 0.0)
        NY[x] = north
        SY[x] = south
        AZ[x] = jnp.where(lane < 127, kh + above, 0.0)
        BZ[x] = jnp.where(lane > 0, kh + below, 0.0)
        D[x] = d
        INV[x] = inv
        U[x] = inv * B[x]
        return carry

    loop(1, last + 2, 2, terms)

    def beside(A, x, r):
        mid = A[x]
        total = EX[x - 1, r] * A[x - 1, r] + EX[x, r] * A[x + 1, r]
        total = total + NY[x, r] * pltpu.roll(mid, ROWS - 1, 0)[r] + SY[x, r] * pltpu.roll(mid, 1, 0)[r]
        part = mid[r]
        return total + AZ[x, r] * pltpu.roll(part, 127, 1) + BZ[x, r] * pltpu.roll(part, 1, 1)

    every = slice(0, ROWS)
    mine = slice(0, T2)

    def solve(src, dst, rc, zs):
        def second(x, carry):
            V[x] = INV[x] * (src[x] + beside(U, x, every))
            return carry

        loop(G - 1, last + 1, 2, second)
        c = coarse(rc)

        def third(x, carry):
            value = INV[x, mine] * (src[x, mine] + beside(V, x, mine))
            for j in range(nc):
                value = value + c[j] * geneo[j, x - G].astype(F32)
            dst[x, mine] = value
            zs[0, pl.ds(x - G, 1)] = value[0:1]
            zs[1, pl.ds(x - G, 1)] = value[15:16]
            return carry

        loop(G, last, 2, third)

    def margin_one(Z, zr):
        def put(x, carry):
            Z[x, 16:24] = jnp.where(sub == 0, zr[0, pl.ds(x - G, 1)], jnp.where(sub == 7, zr[1, pl.ds(x - G, 1)], 0.0))
            return carry

        loop(G, last, 4, put)

    rc_wait1().wait_recv()
    solve(B, Z1, rc1, zs1)
    start(r2)
    arrive(r2)
    margin_one(Z1, zr1)

    zero = jnp.zeros((T2, 128), F32)

    def image_one(x, carry):
        bb, bw, ww = carry
        w = D[x, mine] * Z1[x, mine] - beside(Z1, x, mine)
        b = B[x, mine]
        W[x, mine] = w
        i = x - G
        ws[0, pl.ds(i, 1)] = w[0:1]
        ws[0, pl.ds(nx + i, 1)] = w[1:2]
        ws[1, pl.ds(i, 1)] = w[15:16]
        ws[1, pl.ds(nx + i, 1)] = w[14:15]
        return bb + b * b, bw + b * w, ww + w * w

    bb_part, bw_part, ww_part = loop(G, last, 2, image_one, (zero, zero, zero))
    for i, (x, r) in enumerate(((last - 1, 15), (last - 1, 0), (G, 15), (G, 0))):
        cs[i] = jnp.broadcast_to(W[x, r : r + 1], (8, 128))
    start(r3)
    rc_out[1] = restrict(W)
    rc_wait2 = spread(rc_out.at[1], rc2, 1, in_col)
    row_out[0] = packed((bb_part, bw_part, ww_part), 0)
    ar_wait1 = spread(row_out.at[0], ar1, 2, in_all)
    arrive(r3)

    def put_w(x, carry):
        i = x - G
        tile = jnp.where(sub == 0, wr[0, pl.ds(i, 1)], jnp.where(sub == 1, wr[0, pl.ds(nx + i, 1)], 0.0))
        tile = jnp.where(sub == 7, wr[1, pl.ds(i, 1)], jnp.where(sub == 6, wr[1, pl.ds(nx + i, 1)], tile))
        W[x, 16:24] = tile
        return carry

    loop(G, last, 2, put_w)
    blank_tile = jnp.zeros((8, 128), F32)
    W[G - 2, 16:24] = blank_tile
    W[last + 1, 16:24] = blank_tile
    W[G - 1, 16:24] = jnp.where(sub == 7, cr[0], jnp.where(sub == 0, cr[1], 0.0))
    W[last, 16:24] = jnp.where(sub == 7, cr[2], jnp.where(sub == 0, cr[3], 0.0))

    def first_sweep(x, carry):
        U[x] = INV[x] * W[x]
        return carry

    loop(G - 2, last + 2, 2, first_sweep)
    rc_wait2().wait_recv()
    solve(W, Z2, rc2, zs2)
    start(r4)

    def totals(ar):
        if n_all <= 64:
            total = ar[0]
            for i in range(1, n_all):
                total = total + ar[i]
        else:
            total = lax.fori_loop(1, n_all, lambda i, acc: acc + ar[i], ar[0])
        return [jnp.sum(jnp.where(lane == i, total, 0.0), axis=1, keepdims=True) for i in range(3)]

    ar_wait1().wait_recv()
    bb, bw, ww = totals(ar1)
    h = bw / bb
    arrive(r4)
    margin_one(Z2, zr2)

    def image_two(x, carry):
        wq, qq, bq = carry
        w = W[x, mine]
        image = D[x, mine] * Z2[x, mine] - beside(Z2, x, mine) - h * w
        Y2[x - G] = image
        return wq + w * image, qq + image * image, bq + B[x, mine] * image

    wq_part, qq_part, bq_part = loop(G, last, 2, image_two, (zero, zero, zero))
    row_out[1] = packed((wq_part, qq_part, bq_part), 0)
    ar_wait2 = spread(row_out.at[1], ar2, 3, in_all)
    ar_wait2().wait_recv()
    wq, qq, bq = totals(ar2)
    g11, g12, g22 = ww / bb, wq / bb, qq / bb
    rhs_one, rhs_two = h, bq / bb
    determinant = g11 * g22 - g12 * g12
    y_one = (g22 * rhs_one - g12 * rhs_two) / determinant
    y_two = (g11 * rhs_two - g12 * rhs_one) / determinant
    y_mix = y_one - y_two * h

    def finish(x, carry):
        sol[x - G] = y_mix * Z1[x, mine] + y_two * Z2[x, mine]
        res[x - G] = B[x, mine] - y_one * W[x, mine] - y_two * Y2[x - G]
        return carry

    loop(G, last, 4, finish)
    outs = []
    for i, (src, dst) in enumerate(((sol, sol_hbm), (res, res_hbm))):
        copy = pltpu.make_async_copy(src, dst, load_sem.at[5 + i])
        copy.start()
        outs.append(copy)
    for copy, sends in pending:
        pl.when(sends)(copy.wait_send)
    for wait in (rc_wait1, rc_wait2, ar_wait1, ar_wait2):
        wait().wait_send()
    for copy in outs:
        copy.wait()


def body(n_p, n_q, right_side, conductance, reaction, geneo, coarse_inverse):
    nx, ny, nz = right_side.shape
    assert ny == T2 and nz == 128
    nc = geneo.shape[0]
    ncs = coarse_inverse.shape[1]
    n_all = n_p * n_q
    region = pltpu.VMEM((nx + 2 * G, ROWS, nz), F32)
    field = pltpu.VMEM((nx, ny, nz), F32)
    scratch = [region] * 15 + [
        field,
        pltpu.VMEM(geneo.shape, geneo.dtype),
        pltpu.VMEM(coarse_inverse.shape, F32),
        pltpu.VMEM((nx, 8, nz), F32), pltpu.VMEM((nx, 8, nz), F32),
        pltpu.VMEM((nx + 2 * G, 8, nz), F32), pltpu.VMEM((nx + 2 * G, 8, nz), F32),
    ]
    scratch += [pltpu.VMEM((2, nx, nz), F32)] * 4
    scratch += [pltpu.VMEM((2, 2 * nx, nz), F32)] * 2
    scratch += [pltpu.VMEM((4, 8, nz), F32)] * 2
    scratch += [
        pltpu.VMEM((2, 1, nz), F32), pltpu.VMEM((n_q, 1, nz), F32), pltpu.VMEM((n_q, 1, nz), F32),
        pltpu.VMEM((ncs, nz), F32),
        pltpu.VMEM((2, 1, nz), F32), pltpu.VMEM((n_all, 1, nz), F32), pltpu.VMEM((n_all, 1, nz), F32),
        field, field,
        pltpu.SemaphoreType.DMA((7,)),
        pltpu.SemaphoreType.DMA((28,)), pltpu.SemaphoreType.DMA((28,)),
        pltpu.SemaphoreType.DMA((8,)),
    ]
    out = jax.ShapeDtypeStruct(right_side.shape, F32)
    return pl.pallas_call(
        functools.partial(kernel, n_p, n_q),
        out_shape=(out, out),
        in_specs=[pl.BlockSpec(memory_space=pl.ANY)] * 5,
        out_specs=(pl.BlockSpec(memory_space=pl.ANY),) * 2,
        scratch_shapes=scratch,
        compiler_params=pltpu.CompilerParams(collective_id=0, has_side_effects=True, vmem_limit_bytes=40 * 2**20),
    )(right_side, conductance, reaction, geneo, coarse_inverse)


def solution(mesh):
    return jax.shard_map(
        functools.partial(body, mesh.shape["grp"], mesh.shape["col"]),
        mesh=mesh,
        in_specs=(
            P("grp", "col", None),
            P("grp", "col", None),
            P("grp", "col", None),
            P(None, "grp", "col", None),
            P("grp", None, None),
        ),
        out_specs=(P("grp", "col", None), P("grp", "col", None)),
        check_vma=False,
    )
```

time: 301 us -> 43.3 us (0.14)
  blocking collectives: 180 us -> 0 us
  Pallas kernels: 0 us -> 36.3 us
  starting transfers between devices: 33.8 us -> 0 us
  waiting for transfers between devices: 29.4 us -> 0 us
  other arithmetic: 28.9 us -> 0 us
  between operations: 11.6 us -> 0.65 us
  matrix products: 9.97 us -> 0 us
    psum x4 -> x0, blocking collectives: 161 us -> none  [the longest x2 82.6 us: products(): return lax.psum(values, ('grp', 'col'))]
    pallas_call x0 -> x1, Pallas kernels: none -> 36.3 us  [body(): pl.pallas_call(functools.partial(kernel, n_p, n_q), out_shape=(out, out),...]
    ppermute x16 -> x0, starting transfers between devices: 33.8 us -> none  [the longest x8 23.3 us: padded_2(): lax.ppermute(tail, axis, [(i, (i + 1) % count) for i in range(ends)])]
    ppermute x16 -> x0, waiting for transfers between devices: 29.4 us -> none  [the longest x8 29.2 us: padded_2(): lax.ppermute(head, axis, [((i + 1) % count, i) for i in range(ends)])]
    unnamed x2 -> x0, blocking collectives: 19.1 us -> none
    dot_general x6 -> x0, matrix products: 9.97 us -> none  [the longest x2 5.9 us: precondition(): jnp.einsum('kxyz,xyz->k', vectors, interior(source), precision=highest)]
    add x7 -> x0, other arithmetic: 9.87 us -> none  [the longest x2 3.54 us: precondition(): local_part + jnp.einsum('k,kxyz->xyz', coarse, vectors, precision=highest)]
    reduce_sum x4 -> x0, other arithmetic: 6.66 us -> none  [the longest x1 2.01 us: body(): h32 = jnp.sqrt(squared(jnp.sum(rest * rest)))]
  transfers between devices with their start and end apart: 16 -> 0, of which waited for: 9 -> 0; matrix products, arithmetic and copies ran while one was open for 1% -> 0% of each run, Pallas kernels for 0% -> 0%
where the time goes in v1:
time: 43.3 us; the launch traced here: 43 us
  Pallas kernels  36.3 us (84%)
  local copies, waits for them, and re-layouts  6.09 us (14%)
  between operations  0.65 us (2%)
    pallas_call x1, Pallas kernels, body(): pl.pallas_call(functools.partial(kernel, n_p, n_q), out_shape=(out, out),...  36.3 us
    unnamed x12, local copies, waits for them, and re-layouts  6.09 us

profile of v1, /device:TPU:0, one launch (start us, length us, event | category | flops | bytes accessed | tf_op | source)
XLA Modules:
  0.0 43.0 jit_solution(553764561208097087)
XLA Ops:
  0.6 0.0 copy-start
  0.6 1.1 %copy-done = bf16[6,32,16,128]{3,2,1,0:T(8,128)(2,1)S(1)} copy-done((bf16[6,32,16,128]{3,2,1,0:T(8,128)(2,1)S(1)}, bf16[6,32,16,128]{3,2,1,0:T(8,128)(2,1)}, u32[]{:S(2)}) %copy-start) | copy-done | bytes 786456
  1.8 0.0 copy-start.1
  1.8 0.9 %copy-done.1 = f32[32,16,128]{2,1,0:T(8,128)S(1)} copy-done((f32[32,16,128]{2,1,0:T(8,128)S(1)}, f32[32,16,128]{2,1,0:T(8,128)}, u32[]{:S(2)}) %copy-start.1) | copy-done | bytes 262168
  2.7 0.0 copy-start.2
  2.7 0.9 %copy-done.2 = f32[32,16,128]{2,1,0:T(8,128)S(1)} copy-done((f32[32,16,128]{2,1,0:T(8,128)S(1)}, f32[32,16,128]{2,1,0:T(8,128)}, u32[]{:S(2)}) %copy-start.2) | copy-done | bytes 262168
  3.7 0.0 copy-start.3
  3.7 0.9 %copy-done.3 = f32[32,16,128]{2,1,0:T(8,128)S(1)} copy-done((f32[32,16,128]{2,1,0:T(8,128)S(1)}, f32[32,16,128]{2,1,0:T(8,128)}, u32[]{:S(2)}) %copy-start.3) | copy-done | bytes 262168
  4.6 0.0 copy-start.4
  4.6 0.7 %copy-done.4 = f32[1,24,24]{2,1,0:T(8,128)S(1)} copy-done((f32[1,24,24]{2,1,0:T(8,128)S(1)}, f32[1,24,24]{2,1,0:T(8,128)}, u32[]{:S(2)}) %copy-start.4) | copy-done | bytes 2328
  5.3 36.3 %shard_map.68 = (f32[32,16,128]{2,1,0:T(8,128)S(1)}, f32[32,16,128]{2,1,0:T(8,128)S(1)}) custom-call(f32[32,16,128]{2,1,0:T(8,128)S(1)} %copy-done.1, f32[32,16,128]{2,1,0:T(8,128)S(1)} %copy-done.2, f32[32,16,128]{2,1,0:T(8,128)S(1)} %copy-done.3, bf16[6,32,16,128]{3,2,1,0:T(8,128)(2,1)S(1)} %copy-done, f32[1,24,24]{2,1,0:T(8,128)S(1)} %copy-done.4), custom_call_target="tpu_custom_call" | custom-call | tf_op jit(solution)/shard_map/pallas_call | solution.py:417
  41.6 0.7 %copy.9 = f32[32,16,128]{2,1,0:T(8,128)} copy(f32[32,16,128]{2,1,0:T(8,128)S(1)} %get-tuple-element.4) | data formatting | bytes 524288
  42.3 0.7 %copy.10 = f32[32,16,128]{2,1,0:T(8,128)} copy(f32[32,16,128]{2,1,0:T(8,128)S(1)} %get-tuple-element.5) | data formatting | bytes 524288
Async XLA Ops:
  0.6 1.1 %copy-start = (bf16[6,32,16,128]{3,2,1,0:T(8,128)(2,1)S(1)}, bf16[6,32,16,128]{3,2,1,0:T(8,128)(2,1)}, u32[]{:S(2)}) copy-start(bf16[6,32,16,128]{3,2,1,0:T(8,128)(2,1)} %g_hbm.1) | copy-start | bytes 2359300
  1.8 0.9 %copy-start.1 = (f32[32,16,128]{2,1,0:T(8,128)S(1)}, f32[32,16,128]{2,1,0:T(8,128)}, u32[]{:S(2)}) copy-start(f32[32,16,128]{2,1,0:T(8,128)} %b_hbm.1) | copy-start | bytes 786436
  2.7 0.9 %copy-start.2 = (f32[32,16,128]{2,1,0:T(8,128)S(1)}, f32[32,16,128]{2,1,0:T(8,128)}, u32[]{:S(2)}) copy-start(f32[32,16,128]{2,1,0:T(8,128)} %k_hbm.1) | copy-start | bytes 786436
  3.7 0.9 %copy-start.3 = (f32[32,16,128]{2,1,0:T(8,128)S(1)}, f32[32,16,128]{2,1,0:T(8,128)}, u32[]{:S(2)}) copy-start(f32[32,16,128]{2,1,0:T(8,128)} %s_hbm.1) | copy-start | bytes 786436
  4.6 0.7 %copy-start.4 = (f32[1,24,24]{2,1,0:T(8,128)S(1)}, f32[1,24,24]{2,1,0:T(8,128)}, u32[]{:S(2)}) copy-start(f32[1,24,24]{2,1,0:T(8,128)} %m_hbm.1) | copy-start | bytes 6916

commit v2 on v1

--- a/solution.py
+++ b/solution.py
@@ -180,7 +180,7 @@
             value = src[x, low]
             return tuple(acc + geneo[j, x - G].astype(F32) * value for j, acc in enumerate(carry))
 
-        sums = loop(G, last, 2, step, tuple(jnp.zeros((T2, 128), F32) for _ in range(nc)))
+        sums = loop(G, last, 16, step, tuple(jnp.zeros((T2, 128), F32) for _ in range(nc)))
         return packed(sums, q * nc)
 
     def coarse(rc):
@@ -217,7 +217,7 @@
         B[x, 16:24] = jnp.where(sub < 4, pltpu.roll(plus, 3, 0), pltpu.roll(minus, 5, 0))
         return carry
 
-    loop(0, last + G, 2, fill)
+    loop(0, last + G, 16, fill)
     y_ok = (row < T2) | ((row < T2 + 2) & (q < n_q - 1)) | ((row >= ROWS - 2) & (q > 0))
 
     EX[0] = 0.5 * (K[0] + K[1])
@@ -242,7 +242,7 @@
         U[x] = inv * B[x]
         return carry
 
-    loop(1, last + 2, 2, terms)
+    loop(1, last + 2, 16, terms)
 
     def beside(A, x, r):
         mid = A[x]
@@ -259,7 +259,7 @@
             V[x] = INV[x] * (src[x] + beside(U, x, every))
             return carry
 
-        loop(G - 1, last + 1, 2, second)
+        loop(G - 1, last + 1, 16, second)
         c = coarse(rc)
 
         def third(x, carry):
@@ -271,7 +271,7 @@
             zs[1, pl.ds(x - G, 1)] = value[15:16]
             return carry
 
-        loop(G, last, 2, third)
+        loop(G, last, 16, third)
 
     def margin_one(Z, zr):
         def put(x, carry):
@@ -300,7 +300,7 @@
         ws[1, pl.ds(nx + i, 1)] = w[14:15]
         return bb + b * b, bw + b * w, ww + w * w
 
-    bb_part, bw_part, ww_part = loop(G, last, 2, image_one, (zero, zero, zero))
+    bb_part, bw_part, ww_part = loop(G, last, 16, image_one, (zero, zero, zero))
     for i, (x, r) in enumerate(((last - 1, 15), (last - 1, 0), (G, 15), (G, 0))):
         cs[i] = jnp.broadcast_to(W[x, r : r + 1], (8, 128))
     start(r3)
@@ -317,7 +317,7 @@
         W[x, 16:24] = tile
         return carry
 
-    loop(G, last, 2, put_w)
+    loop(G, last, 16, put_w)
     blank_tile = jnp.zeros((8, 128), F32)
     W[G - 2, 16:24] = blank_tile
     W[last + 1, 16:24] = blank_tile
@@ -328,7 +328,7 @@
         U[x] = INV[x] * W[x]
         return carry
 
-    loop(G - 2, last + 2, 2, first_sweep)
+    loop(G - 2, last + 2, 16, first_sweep)
     rc_wait2().wait_recv()
     solve(W, Z2, rc2, zs2)
     start(r4)
@@ -355,7 +355,7 @@
         Y2[x - G] = image
         return wq + w * image, qq + image * image, bq + B[x, mine] * image
 
-    wq_part, qq_part, bq_part = loop(G, last, 2, image_two, (zero, zero, zero))
+    wq_part, qq_part, bq_part = loop(G, last, 16, image_two, (zero, zero, zero))
     row_out[1] = packed((wq_part, qq_part, bq_part), 0)
     ar_wait2 = spread(row_out.at[1], ar2, 3, in_all)
     ar_wait2().wait_recv()
@@ -420,7 +420,7 @@
         in_specs=[pl.BlockSpec(memory_space=pl.ANY)] * 5,
         out_specs=(pl.BlockSpec(memory_space=pl.ANY),) * 2,
         scratch_shapes=scratch,
-        compiler_params=pltpu.CompilerParams(collective_id=0, has_side_effects=True, vmem_limit_bytes=40 * 2**20),
+        compiler_params=pltpu.CompilerParams(collective_id=0, has_side_effects=True, vmem_limit_bytes=67043328),
     )(right_side, conductance, reaction, geneo, coarse_inverse)
 
 

time: 43.3 us -> 32.7 us (0.76)
  Pallas kernels: 36.3 us -> 29.4 us
  local copies, waits for them, and re-layouts: 6.09 us -> 2.42 us
    pallas_call x1, Pallas kernels: 36.3 us -> 29.4 us  [body(): pl.pallas_call(functools.partial(kernel, n_p, n_q), out_shape=(out, out),...]
    unnamed x12 -> x4, local copies, waits for them, and re-layouts: 6.09 us -> 2.42 us
where the time goes in v2:
time: 32.7 us; the launch traced here: 32.5 us
  Pallas kernels  29.4 us (90%)
  local copies, waits for them, and re-layouts  2.42 us (7%)
  between operations  0.65 us (2%)
    pallas_call x1, Pallas kernels, body(): pl.pallas_call(functools.partial(kernel, n_p, n_q), out_shape=(out, out),...  29.4 us
    unnamed x4, local copies, waits for them, and re-layouts  2.42 us

profile of v2, /device:TPU:0, one launch (start us, length us, event | category | flops | bytes accessed | tf_op | source)
XLA Modules:
  0.0 32.5 jit_solution(1571513308801650394)
XLA Ops:
  0.6 29.4 %shard_map.68 = (f32[32,16,128]{2,1,0:T(8,128)}, f32[32,16,128]{2,1,0:T(8,128)}) custom-call(f32[32,16,128]{2,1,0:T(8,128)} %b_hbm.1, f32[32,16,128]{2,1,0:T(8,128)} %k_hbm.1, f32[32,16,128]{2,1,0:T(8,128)} %s_hbm.1, bf16[6,32,16,128]{3,2,1,0:T(8,128)(2,1)} %g_hbm.1, f32[1,24,24]{2,1,0:T(8,128)} %m_hbm.1), custom_call_target="tpu_custom_call" | custom-call | tf_op jit(solution)/shard_map/pallas_call | solution.py:417
  30.1 0.0 copy-start
  30.1 1.7 %copy.9 = f32[32,16,128]{2,1,0:T(8,128)} copy(f32[32,16,128]{2,1,0:T(8,128)} %get-tuple-element.4) | data formatting | bytes 524288
  31.8 0.0 copy-done
  31.8 0.7 %copy.10 = f32[32,16,128]{2,1,0:T(8,128)} copy(f32[32,16,128]{2,1,0:T(8,128)S(1)} %copy-done) | data formatting | bytes 524288
Async XLA Ops:
  30.1 1.7 %copy-start = (f32[32,16,128]{2,1,0:T(8,128)S(1)}, f32[32,16,128]{2,1,0:T(8,128)}, u32[]{:S(2)}) copy-start(f32[32,16,128]{2,1,0:T(8,128)} %get-tuple-element.5) | copy-start | bytes 786436

commit v3 on v2

--- a/solution.py
+++ b/solution.py
@@ -138,6 +138,13 @@
     for items in (r1, r2, r3, r4):
         blank(items)
 
+    def clear(x, carry):
+        for Z in (Z1, Z2):
+            Z[x, 16:24] = jnp.zeros((8, 128), F32)
+        return carry
+
+    loop(G, last, 16, clear)
+
     def spread(src, dst, i, devices):
         count, slot, where = devices
 
@@ -254,7 +261,7 @@
     every = slice(0, ROWS)
     mine = slice(0, T2)
 
-    def solve(src, dst, rc, zs):
+    def solve(src, dst, rc, zs, faces):
         def second(x, carry):
             V[x] = INV[x] * (src[x] + beside(U, x, every))
             return carry
@@ -271,26 +278,41 @@
             zs[1, pl.ds(x - G, 1)] = value[15:16]
             return carry
 
-        loop(G, last, 16, third)
-
-    def margin_one(Z, zr):
-        def put(x, carry):
-            Z[x, 16:24] = jnp.where(sub == 0, zr[0, pl.ds(x - G, 1)], jnp.where(sub == 7, zr[1, pl.ds(x - G, 1)], 0.0))
+        third(G, ())
+        third(last - 1, ())
+        start(faces[:2])
+        loop(G + 1, last - 1, 15, third)
+        start(faces[2:])
+
+    def image(Z, put, faces):
+        def step(x, carry):
+            put(x, D[x, mine] * Z[x, mine] - beside(Z, x, mine))
             return carry
 
-        loop(G, last, 4, put)
+        loop(G + 1, last - 1, 15, step)
+        arrive(faces)
+        step(G, ())
+        step(last - 1, ())
+
+    def with_faces(value, x, zr):
+        i = pl.ds(x - G, 1)
+        top = jnp.where(sub == 0, SY[x, 0:8] * zr[1, i], 0.0)
+        bottom = jnp.where(sub == 7, NY[x, 8:16] * zr[0, i], 0.0)
+        return value - jnp.concatenate([top, bottom], axis=0)
 
     rc_wait1().wait_recv()
-    solve(B, Z1, rc1, zs1)
-    start(r2)
-    arrive(r2)
-    margin_one(Z1, zr1)
+    solve(B, Z1, rc1, zs1, r2)
+
+    def put_one(x, value):
+        W[x, mine] = value
+
+    image(Z1, put_one, r2)
 
     zero = jnp.zeros((T2, 128), F32)
 
     def image_one(x, carry):
         bb, bw, ww = carry
-        w = D[x, mine] * Z1[x, mine] - beside(Z1, x, mine)
+        w = with_faces(W[x, mine], x, zr1)
         b = B[x, mine]
         W[x, mine] = w
         i = x - G
@@ -330,8 +352,7 @@
 
     loop(G - 2, last + 2, 16, first_sweep)
     rc_wait2().wait_recv()
-    solve(W, Z2, rc2, zs2)
-    start(r4)
+    solve(W, Z2, rc2, zs2, r4)
 
     def totals(ar):
         if n_all <= 64:
@@ -342,18 +363,21 @@
             total = lax.fori_loop(1, n_all, lambda i, acc: acc + ar[i], ar[0])
         return [jnp.sum(jnp.where(lane == i, total, 0.0), axis=1, keepdims=True) for i in range(3)]
 
+
+    def put_two(x, value):
+        Y2[x - G] = value
+
+    image(Z2, put_two, r4)
     ar_wait1().wait_recv()
     bb, bw, ww = totals(ar1)
     h = bw / bb
-    arrive(r4)
-    margin_one(Z2, zr2)
 
     def image_two(x, carry):
         wq, qq, bq = carry
         w = W[x, mine]
-        image = D[x, mine] * Z2[x, mine] - beside(Z2, x, mine) - h * w
-        Y2[x - G] = image
-        return wq + w * image, qq + image * image, bq + B[x, mine] * image
+        value = with_faces(Y2[x - G], x, zr2) - h * w
+        Y2[x - G] = value
+        return wq + w * value, qq + value * value, bq + B[x, mine] * value
 
     wq_part, qq_part, bq_part = loop(G, last, 16, image_two, (zero, zero, zero))
     row_out[1] = packed((wq_part, qq_part, bq_part), 0)

time: 32.7 us -> 31.8 us (0.972)
  Pallas kernels: 29.4 us -> 28.6 us
    pallas_call x1, Pallas kernels: 29.4 us -> 28.6 us  [body(): pl.pallas_call(functools.partial(kernel, n_p, n_q), out_shape=(out, out),...]
where the time goes in v3:
time: 31.8 us; the launch traced here: 31.7 us
  Pallas kernels  28.6 us (90%)
  local copies, waits for them, and re-layouts  2.42 us (8%)
  between operations  0.65 us (2%)
    pallas_call x1, Pallas kernels, body(): pl.pallas_call(functools.partial(kernel, n_p, n_q), out_shape=(out, out),...  28.6 us
    unnamed x4, local copies, waits for them, and re-layouts  2.42 us

profile of v3, /device:TPU:0, one launch (start us, length us, event | category | flops | bytes accessed | tf_op | source)
XLA Modules:
  0.0 31.7 jit_solution(17148233835576572299)
XLA Ops:
  0.6 28.6 %shard_map.68 = (f32[32,16,128]{2,1,0:T(8,128)}, f32[32,16,128]{2,1,0:T(8,128)}) custom-call(f32[32,16,128]{2,1,0:T(8,128)} %b_hbm.1, f32[32,16,128]{2,1,0:T(8,128)} %k_hbm.1, f32[32,16,128]{2,1,0:T(8,128)} %s_hbm.1, bf16[6,32,16,128]{3,2,1,0:T(8,128)(2,1)} %g_hbm.1, f32[1,24,24]{2,1,0:T(8,128)} %m_hbm.1), custom_call_target="tpu_custom_call" | custom-call | tf_op jit(solution)/shard_map/pallas_call | solution.py:441
  29.2 0.0 copy-start
  29.3 1.7 %copy.9 = f32[32,16,128]{2,1,0:T(8,128)} copy(f32[32,16,128]{2,1,0:T(8,128)} %get-tuple-element.4) | data formatting | bytes 524288
  31.0 0.0 copy-done
  31.0 0.7 %copy.10 = f32[32,16,128]{2,1,0:T(8,128)} copy(f32[32,16,128]{2,1,0:T(8,128)S(1)} %copy-done) | data formatting | bytes 524288
Async XLA Ops:
  29.2 1.7 %copy-start = (f32[32,16,128]{2,1,0:T(8,128)S(1)}, f32[32,16,128]{2,1,0:T(8,128)}, u32[]{:S(2)}) copy-start(f32[32,16,128]{2,1,0:T(8,128)} %get-tuple-element.5) | copy-start | bytes 786436
